TPU v7x, 32 devices: a whole 2x2x4 slice. The times are simulated.
32 devices in a mesh: ctx: 8 (over z, x), head: 4 (over y, core).
Axes of the slice: x: 2, y: 2, z: 4, core: 2. Of those that a mesh axis runs over, the one named last changes fastest.
Arguments:
- queries: bfloat16 [4096, 3072], P('ctx', 'head'), may hold values from -26 to 26
- keys: bfloat16 [4096, 3072], P('ctx', 'head'), may hold values from -26 to 26
- values: bfloat16 [4096, 3072], P('ctx', 'head'), may hold values from -6 to 6
- kv_tiles: int32 [32, 12], replicated, may hold values from 0 to 31, as said below
- out_weight: bfloat16 [3072, 3072], P('head'), may hold values from -0.109375 to 0.109375
Outputs:
- attended: bfloat16 [4096, 3072], P(('ctx', 'head'))
Inputs may be any that keep to these rules, and one draw needn't show every extreme that they name: `kv_tiles`: every row i lists tile i itself; entries may repeat. A listed tile lies on a device (tile index // 4) within 2 of the device of row i, and from every other device within 2 the rows of one device read between 1 and 2 distinct tiles.
All inputs are finite; a program needn't handle non-finite values.
Results may differ from a plain program's by a relative error of at most 0.009.
Values may be sent and summed in bfloat16 or wider, within the bound.
A program may use at most 128 MiB of HBM per device.

v0:
```python
import jax
import jax.numpy as jnp
from jax import lax
from jax.sharding import PartitionSpec as P

HD = 128
TILE = 128
REACH = 2


def shifted(value, axis, by):
    peers = lax.axis_size(axis)
    pairs = [(i, i + by) for i in range(peers) if 0 <= i + by < peers]
    return lax.ppermute(value, axis, pairs)


def body(queries, keys, values, kv_tiles, out_weight):
    tok_rows = queries.shape[0]
    columns = queries.shape[1]
    heads_here = columns // HD
    tile_count = tok_rows // TILE
    device = lax.axis_index("ctx")
    devices = lax.axis_size("ctx")
    stacked = jnp.stack([keys, values])
    offsets = [offset for offset in range(-REACH, REACH + 1) if offset != 0]
    pieces = [stacked]
    id_parts = [device * tile_count + jnp.arange(tile_count, dtype=jnp.int32)]
    for offset in offsets:
        received = shifted(stacked, "ctx", -offset)
        source = device + offset
        in_range = (source >= 0) & (source < devices)
        pieces.append(received)
        id_parts.append(
            jnp.where(in_range, source * tile_count + jnp.arange(tile_count, dtype=jnp.int32), -1)
        )
    buffer = jnp.concatenate(pieces, axis=1)
    tile_ids = jnp.concatenate(id_parts)
    key_tiles = tile_ids.shape[0]
    own_lists = lax.dynamic_slice_in_dim(kv_tiles, device * tile_count, tile_count, 0)
    allowed = jnp.any(own_lists[:, None, :] == tile_ids[None, :, None], axis=2)
    allowed_keys = jnp.broadcast_to(
        allowed[:, None, :, None], (tile_count, TILE, key_tiles, TILE)
    ).reshape(tok_rows, key_tiles * TILE)
    query_heads = queries.reshape(tok_rows, heads_here, HD)
    key_heads = buffer[0].reshape(key_tiles * TILE, heads_here, HD)
    value_heads = buffer[1].reshape(key_tiles * TILE, heads_here, HD)
    scores = jnp.einsum(
        "qhd,khd->hqk", query_heads, key_heads, preferred_element_type=jnp.float32
    ) * HD ** (-0.5)
    masked = jnp.where(allowed_keys[None], scores, -jnp.inf)
    row_max = jnp.max(masked, axis=-1, keepdims=True)
    weights = jnp.where(allowed_keys[None], jnp.exp(masked - row_max), 0.0)
    denominator = jnp.sum(weights, axis=-1)
    rounded = weights.astype(jnp.bfloat16)
    summed = jnp.einsum("hqk,khd->qhd", rounded, value_heads, preferred_element_type=jnp.float32)
    context = (
        (summed / jnp.transpose(denominator)[:, :, None])
        .astype(jnp.bfloat16)
        .reshape(tok_rows, columns)
    )
    return lax.psum_scatter(
        jnp.dot(context, out_weight, preferred_element_type=jnp.float32).astype(jnp.bfloat16),
        "head",
        scatter_dimension=0,
        tiled=True,
    )


def solution(mesh):
    return jax.shard_map(
        body,
        mesh=mesh,
        in_specs=(P("ctx", "head"), P("ctx", "head"), P("ctx", "head"), P(), P("head", None)),
        out_specs=P(("ctx", "head"), None),
        check_vma=False,
    )
```

profile of v0, /device:TPU:0, one launch (start us, length us, event | category | flops | bytes accessed | tf_op | source)
XLA Modules:
  0.0 180.6 jit_solution(7597886839423358261)
XLA Ops:
  6.5 0.0 copy-start
  6.5 0.0 reduce-scatter.2.cloned.1.call-start
  6.5 1.4 copy.17
  8.0 1.4 copy.18
  9.4 2.0 %pad_maximum_fusion = (bf16[2,512,768]{1,2,0:T(8,128)(2,1)}, bf16[2,2560,768]{1,2,0:T(8,128)(2,1)}) fusion(bf16[1,512,768]{1,2,0:T(8,128)(2,1)S(1)} %bitcast.41, bf16[1,512,768]{1,2,0:T(8,128)(2,1)S(1)} %bitcast.40), kind=kLoop, calls=%fused_computation.12 | loop fusion | flops 3145727 | bytes 4718592 | tf_op jit(solution)/shard_map/stack | solution.py:24
  11.4 6.1 %collective-permute-start = (bf16[2,512,768]{1,2,0:T(8,128)(2,1)}, bf16[2,512,768]{1,2,0:T(8,128)(2,1)}, u32[]{:S(2)}, u32[]{:S(2)}) collective-permute-start(bf16[2,512,768]{1,2,0:T(8,128)(2,1)} %get-tuple-element.7), channel_id=1, source_target_pairs={{0,8},{4,12},{8,16},{12,20},{16,24},{20,28},{1,9},{5,13},{9,17},{1... | collective-permute-start | bytes 4718600 | tf_op jit(solution)/shard_map/ppermute | solution.py:14
  17.5 4.6 %collective-permute-start.1 = (bf16[2,512,768]{1,2,0:T(8,128)(2,1)}, bf16[2,512,768]{1,2,0:T(8,128)(2,1)}, u32[]{:S(2)}, u32[]{:S(2)}) collective-permute-start(bf16[2,512,768]{1,2,0:T(8,128)(2,1)} %get-tuple-element.7), channel_id=1, source_target_pairs={{0,4},{4,8},{8,12},{12,16},{16,20},{20,24},{24,28},{1,5},{5,9},{9,... | collective-permute-start | bytes 4718600 | tf_op jit(solution)/shard_map/ppermute | solution.py:14
  22.1 1.3 collective-permute-start.2
  23.4 1.3 collective-permute-start.3
  24.7 0.1 concatenate.7
  24.8 0.0 copy-done
  24.8 0.1 constant_dynamic-slice_fusion
  24.9 0.1 compare_reduce_fusion
  25.0 0.1 copy.19
  25.1 2.3 %copy.20 = bf16[512,768]{0,1:T(8,128)(2,1)} copy(bf16[512,768]{1,0:T(8,128)(2,1)} %param.5) | data formatting | bytes 1572864 | tf_op args[0]
  27.4 0.7 broadcast_in_dim.38
  28.1 1.7 copy.29
  29.9 20.4 %collective-permute-done = bf16[2,512,768]{1,2,0:T(8,128)(2,1)} collective-permute-done((bf16[2,512,768]{1,2,0:T(8,128)(2,1)}, bf16[2,512,768]{1,2,0:T(8,128)(2,1)}, u32[]{:S(2)}, u32[]{:S(2)}) %collective-permute-start) | collective-permute-done | bytes 1572896 | tf_op jit(solution)/shard_map/ppermute | solution.py:14
  50.3 2.7 %constant_dynamic-update-slice_fusion.3 = bf16[2,2560,768]{1,2,0:T(8,128)(2,1)} fusion(bf16[2,2560,768]{1,2,0:T(8,128)(2,1)} %get-tuple-element.8, bf16[2,512,768]{1,2,0:T(8,128)(2,1)} %collective-permute-done), kind=kLoop, calls=%fused_computation.19 | loop fusion | bytes 3145728
  53.0 35.3 %collective-permute-done.1 = bf16[2,512,768]{1,2,0:T(8,128)(2,1)} collective-permute-done((bf16[2,512,768]{1,2,0:T(8,128)(2,1)}, bf16[2,512,768]{1,2,0:T(8,128)(2,1)}, u32[]{:S(2)}, u32[]{:S(2)}) %collective-permute-start.1) | collective-permute-done | bytes 1572896 | tf_op jit(solution)/shard_map/ppermute | solution.py:14
  88.3 2.7 %constant_dynamic-update-slice_fusion.2 = bf16[2,2560,768]{1,2,0:T(8,128)(2,1)} fusion(bf16[2,2560,768]{1,2,0:T(8,128)(2,1)} %constant_dynamic-update-slice_fusion.3, bf16[2,512,768]{1,2,0:T(8,128)(2,1)} %collective-permute-done.1), kind=kLoop, calls=%fused_computation.18 | loop fusion | bytes 3145728
  91.0 0.0 collective-permute-done.2
  91.0 1.4 constant_dynamic-update-slice_fusion.1
  92.4 0.0 collective-permute-done.3
  92.4 1.3 constant_dynamic-update-slice_fusion
  93.7 0.0 copy-start.1
  93.7 0.0 copy-start.2
  93.7 5.8 %fusion.14 = (bf16[1,2560,768]{1,2,0:T(8,128)(2,1)}, bf16[1,2560,768]{1,2,0:T(8,128)(2,1)}) fusion(bf16[2,2560,768]{1,2,0:T(8,128)(2,1)} %constant_dynamic-update-slice_fusion), kind=kLoop, calls=%fused_computation.29 | loop fusion | bytes 15728640 | tf_op jit(solution)/shard_map/slice | solution.py:45
  99.5 0.0 copy-done.1
  99.5 0.0 copy-done.2
  99.5 20.9 %fusion.15 = (f32[6,512]{1,0:T(8,128)S(1)}, bf16[6,512,2560]{1,2,0:T(8,128)(2,1)}) fusion(pred[512,2560]{0,1:T(8,128)(4,1)S(1)} %bitcast.42, bf16[2560,6,128]{0,2,1:T(8,128)(2,1)} %bitcast.39, bf16[512,6,128]{0,2,1:T(8,128)(2,1)S(1)} %bitcast.43), kind=kOutput, calls=%fused_computation.30 | convolution fusion | flops 2060454400 | bytes 21770240 | tf_op jit(solution)/shard_map/sub | solution.py:52
  120.4 8.9 %fusion.9 = bf16[512,6,128]{0,2,1:T(8,128)(2,1)S(1)} fusion(bf16[2560,6,128]{0,2,1:T(8,128)(2,1)} %bitcast.38, bf16[6,512,2560]{1,2,0:T(8,128)(2,1)} %get-tuple-element.10, f32[512,6]{0,1:T(8,128)S(1)} %bitcast.45), kind=kOutput, calls=%fused_computation.14 | convolution fusion | flops 2014052352 | bytes 20459520 | tf_op jit(solution)/shard_map/hqk,khd->qhd/dot_general | solution.py:55
  129.3 6.4 %convolution_convert_fusion = bf16[512,3072]{1,0:T(8,128)(2,1)} fusion(bf16[512,768]{0,1:T(8,128)(2,1)S(1)} %bitcast.44, bf16[768,3072]{1,0:T(8,128)(2,1)} %param.9), kind=kOutput, calls=%fused_computation.10 | convolution fusion | flops 2417491968 | bytes 8650752 | tf_op jit(solution)/shard_map/dot_general | solution.py:62
  135.6 0.0 reduce-scatter.2.cloned.1.call-update
  135.7 38.1 %reduce-scatter.2.cloned.1.call-done = bf16[128,3072]{1,0:T(8,128)(2,1)} async-done(((bf16[512,3072]{1,0:T(8,128)(2,1)}), bf16[128,3072]{1,0:T(8,128)(2,1)}) %reduce-scatter.2.cloned.1.call-update) | async-done | bytes 786448 | tf_op jit(solution)/shard_map/reduce_scatter | solution.py:61
  (3 shorter events, 0.0 us)
Async XLA Ops:
  6.5 18.3 %copy-start = (s32[32,12]{0,1:T(8,128)S(1)}, s32[32,12]{0,1:T(8,128)}, u32[]{:S(2)}) copy-start(s32[32,12]{0,1:T(8,128)} %param.8) | copy-start | bytes 4612
  6.5 167.2 %reduce-scatter.2.cloned.1.call-start = ((), (), s32[]{:S(2)}) async-start(), calls=%async_computation.1 | async-start | bytes 3932160 | tf_op jit(solution)/shard_map/reduce_scatter | solution.py:61
  11.4 38.9 %collective-permute-start = (bf16[2,512,768]{1,2,0:T(8,128)(2,1)}, bf16[2,512,768]{1,2,0:T(8,128)(2,1)}, u32[]{:S(2)}, u32[]{:S(2)}) collective-permute-start(bf16[2,512,768]{1,2,0:T(8,128)(2,1)} %get-tuple-element.7), channel_id=1, source_target_pairs={{0,8},{4,12},{8,16},{12,20},{16,24},{20,28},{1,9},{5,13},{9,17},{1... | collective-permute-start | bytes 4718600 | tf_op jit(solution)/shard_map/ppermute | solution.py:14
  17.5 70.8 %collective-permute-start.1 = (bf16[2,512,768]{1,2,0:T(8,128)(2,1)}, bf16[2,512,768]{1,2,0:T(8,128)(2,1)}, u32[]{:S(2)}, u32[]{:S(2)}) collective-permute-start(bf16[2,512,768]{1,2,0:T(8,128)(2,1)} %get-tuple-element.7), channel_id=1, source_target_pairs={{0,4},{4,8},{8,12},{12,16},{16,20},{20,24},{24,28},{1,5},{5,9},{9,... | collective-permute-start | bytes 4718600 | tf_op jit(solution)/shard_map/ppermute | solution.py:14
  22.1 68.9 %collective-permute-start.2 = (bf16[2,512,768]{1,2,0:T(8,128)(2,1)}, bf16[2,512,768]{1,2,0:T(8,128)(2,1)S(1)}, u32[]{:S(2)}, u32[]{:S(2)}) collective-permute-start(bf16[2,512,768]{1,2,0:T(8,128)(2,1)} %get-tuple-element.7), channel_id=1, source_target_pairs={{4,0},{8,4},{12,8},{16,12},{20,16},{24,20},{28,24},{5,1},{9,5},{13... | collective-permute-start | bytes 4718600 | tf_op jit(solution)/shard_map/ppermute | solution.py:14
  23.4 69.0 %collective-permute-start.3 = (bf16[2,512,768]{1,2,0:T(8,128)(2,1)}, bf16[2,512,768]{1,2,0:T(8,128)(2,1)S(1)}, u32[]{:S(2)}, u32[]{:S(2)}) collective-permute-start(bf16[2,512,768]{1,2,0:T(8,128)(2,1)} %get-tuple-element.7), channel_id=1, source_target_pairs={{8,0},{12,4},{16,8},{20,12},{24,16},{28,20},{9,1},{13,5},{17,9},{2... | collective-permute-start | bytes 4718600 | tf_op jit(solution)/shard_map/ppermute | solution.py:14
  93.7 5.8 %copy-start.1 = (pred[320,8,4,128]{3,1,2,0:T(8,128)(4,1)S(1)}, pred[320,8,4,128]{3,1,2,0:T(8,128)(4,1)}, u32[]{:S(2)}) copy-start(pred[320,8,4,128]{3,1,2,0:T(8,128)(4,1)} %copy.29) | copy-start | bytes 3932164
  93.7 5.8 %copy-start.2 = (bf16[512,768]{0,1:T(8,128)(2,1)S(1)}, bf16[512,768]{0,1:T(8,128)(2,1)}, u32[]{:S(2)}) copy-start(bf16[512,768]{0,1:T(8,128)(2,1)} %copy.20) | copy-start | bytes 2359300
Sparse Core Ops, SparseCore 0:
  135.8 37.9 reduce-scatter.1
where the time goes:
time: 181 us
  waiting for transfers between devices  93.8 us (52%)
  matrix products  36.2 us (20%)
  local copies, waits for them, and re-layouts  21.8 us (12%)
  between operations  13.5 us (7%)
  starting transfers between devices  13.2 us (7%)
  other arithmetic  2.14 us (1%)
    ppermute x4, waiting for transfers between devices, shifted(): return lax.ppermute(value, axis, pairs)  55.7 us
    reduce_scatter x1, waiting for transfers between devices, body(): lax.psum_scatter(jnp.dot(context, out_weight, preferred_element_type=jnp....  38.1 us
    sub x1, matrix products, body(): weights = jnp.where(allowed_keys[None], jnp.exp(masked - row_max), 0.0)  20.9 us
    unnamed x13, local copies, waits for them, and re-layouts  13.7 us
    ppermute x4, starting transfers between devices, shifted(): return lax.ppermute(value, axis, pairs)  13.2 us
    dot_general x1, matrix products, body(): jnp.einsum('hqk,khd->qhd', rounded, value_heads, preferred_element_type=j...  8.86 us
    dot_general x1, matrix products, body(): jnp.dot(context, out_weight, preferred_element_type=jnp.float32)  6.38 us
    slice x1, local copies, waits for them, and re-layouts, body(): key_heads = buffer[0].reshape(key_tiles * TILE, heads_here, HD)  5.78 us
  transfers between devices with their start and end apart: 5, of which 3 were waited for; matrix products, arithmetic and copies ran while one was open for 7% of the time, Pallas kernels for 0%

commit v1 on v0

--- a/solution.py
+++ b/solution.py
@@ -6,6 +6,7 @@
 HD = 128
 TILE = 128
 REACH = 2
+PAIR = 2
 
 
 def shifted(value, axis, by):
@@ -14,32 +15,44 @@
     return lax.ppermute(value, axis, pairs)
 
 
+def extremes(kv_tiles, reader, owner, per, devices):
+    rows = lax.dynamic_slice_in_dim(kv_tiles, jnp.clip(reader, 0, devices - 1) * per, per, 0)
+    inside = (rows // per == owner) & (reader >= 0) & (reader < devices)
+    least = jnp.min(jnp.where(inside, rows % per, per - 1))
+    most = jnp.max(jnp.where(inside, rows % per, 0))
+    return least, most, jnp.any(inside)
+
+
 def body(queries, keys, values, kv_tiles, out_weight):
-    tok_rows = queries.shape[0]
-    columns = queries.shape[1]
+    tok_rows, columns = queries.shape
     heads_here = columns // HD
-    tile_count = tok_rows // TILE
+    per = tok_rows // TILE
     device = lax.axis_index("ctx")
     devices = lax.axis_size("ctx")
     stacked = jnp.stack([keys, values])
-    offsets = [offset for offset in range(-REACH, REACH + 1) if offset != 0]
     pieces = [stacked]
-    id_parts = [device * tile_count + jnp.arange(tile_count, dtype=jnp.int32)]
-    for offset in offsets:
-        received = shifted(stacked, "ctx", -offset)
+    id_parts = [device * per + jnp.arange(per, dtype=jnp.int32)]
+    for offset in [o for o in range(-REACH, REACH + 1) if o]:
+        least, most, _ = extremes(kv_tiles, device - offset, device, per, devices)
+        packed = jnp.concatenate(
+            [lax.dynamic_slice_in_dim(stacked, t * TILE, TILE, 1) for t in (least, most)], axis=1
+        )
+        pieces.append(shifted(packed, "ctx", -offset))
         source = device + offset
-        in_range = (source >= 0) & (source < devices)
-        pieces.append(received)
+        least, most, found = extremes(kv_tiles, device, source, per, devices)
         id_parts.append(
-            jnp.where(in_range, source * tile_count + jnp.arange(tile_count, dtype=jnp.int32), -1)
+            jnp.stack([
+                jnp.where(found, source * per + least, -1),
+                jnp.where(found & (most != least), source * per + most, -1),
+            ])
         )
     buffer = jnp.concatenate(pieces, axis=1)
     tile_ids = jnp.concatenate(id_parts)
     key_tiles = tile_ids.shape[0]
-    own_lists = lax.dynamic_slice_in_dim(kv_tiles, device * tile_count, tile_count, 0)
+    own_lists = lax.dynamic_slice_in_dim(kv_tiles, device * per, per, 0)
     allowed = jnp.any(own_lists[:, None, :] == tile_ids[None, :, None], axis=2)
     allowed_keys = jnp.broadcast_to(
-        allowed[:, None, :, None], (tile_count, TILE, key_tiles, TILE)
+        allowed[:, None, :, None], (per, TILE, key_tiles, TILE)
     ).reshape(tok_rows, key_tiles * TILE)
     query_heads = queries.reshape(tok_rows, heads_here, HD)
     key_heads = buffer[0].reshape(key_tiles * TILE, heads_here, HD)

time: 181 us -> 140 us (0.77)
  waiting for transfers between devices: 93.8 us -> 46.2 us
  between operations: 13.5 us -> 33.6 us
  matrix products: 36.2 us -> 24.3 us
  local copies, waits for them, and re-layouts: 21.8 us -> 11.3 us
  other arithmetic: 2.14 us -> 11.8 us
    ppermute x4, waiting for transfers between devices: 55.7 us -> 10.7 us  [shifted(): return lax.ppermute(value, axis, pairs)]
    sub x1, matrix products: 20.9 us -> 12.9 us  [body(): weights = jnp.where(allowed_keys[None], jnp.exp(masked - row_max), 0.0)]
    unnamed x13 -> x17, local copies, waits for them, and re-layouts: 13.7 us -> 7.72 us
    slice x1, local copies, waits for them, and re-layouts: 5.78 us -> 1.7 us  [body(): key_heads = buffer[0].reshape(key_tiles * TILE, heads_here, HD)]
    dot_general x1, matrix products: 8.86 us -> 5.07 us  [body(): jnp.einsum('hqk,khd->qhd', rounded, value_heads, preferred_element_type=j...]
    reduce_or x0 -> x3, other arithmetic: none -> 3.63 us  [extremes(): return (least, most, jnp.any(inside))]
    concatenate x0 -> x4, other arithmetic: none -> 3 us  [body(): jnp.concatenate([lax.dynamic_slice_in_dim(stacked, t * TILE, TILE, 1) for...]
    reduce_scatter x1, waiting for transfers between devices: 38.1 us -> 35.5 us  [body(): lax.psum_scatter(jnp.dot(context, out_weight, preferred_element_type=jnp....]
  transfers between devices with their start and end apart: 5 -> 5, of which waited for: 3 -> 2; matrix products, arithmetic and copies ran while one was open for 7% -> 9% of each run, Pallas kernels for 0% -> 0%
where the time goes in v1:
time: 140 us; the launch traced here: 139 us
  waiting for transfers between devices  46.2 us (33%)
  between operations  33.6 us (24%)
  matrix products  24.3 us (17%)
  starting transfers between devices  12.1 us (9%)
  other arithmetic  11.8 us (8%)
  local copies, waits for them, and re-layouts  11.3 us (8%)
    reduce_scatter x1, waiting for transfers between devices, body(): lax.psum_scatter(jnp.dot(context, out_weight, preferred_element_type=jnp....  35.5 us
    sub x1, matrix products, body(): weights = jnp.where(allowed_keys[None], jnp.exp(masked - row_max), 0.0)  12.9 us
    ppermute x4, starting transfers between devices, shifted(): return lax.ppermute(value, axis, pairs)  12.1 us
    ppermute x4, waiting for transfers between devices, shifted(): return lax.ppermute(value, axis, pairs)  10.7 us
    unnamed x17, local copies, waits for them, and re-layouts  7.72 us
    dot_general x1, matrix products, body(): jnp.dot(context, out_weight, preferred_element_type=jnp.float32)  6.37 us
    dot_general x1, matrix products, body(): jnp.einsum('hqk,khd->qhd', rounded, value_heads, preferred_element_type=j...  5.07 us
    reduce_or x3, other arithmetic, extremes(): return (least, most, jnp.any(inside))  3.63 us
  transfers between devices with their start and end apart: 5, of which 2 were waited for; matrix products, arithmetic and copies ran while one was open for 9% of the time, Pallas kernels for 0%

profile of v1, /device:TPU:0, one launch (start us, length us, event | category | flops | bytes accessed | tf_op | source)
XLA Modules:
  0.0 139.4 jit_solution(11246110162753473133)
XLA Ops:
  6.5 0.0 copy-start
  6.5 0.0 reduce-scatter.2.cloned.1.call-start
  6.5 0.9 and_and_fusion.7
  7.4 2.2 %fusion.32 = (pred[]{:T(512)}, pred[4,12]{0,1:T(8,128)(4,1)}, s32[4,12]{0,1:T(8,128)S(1)}, pred[4,12]{0,1:T(8,128)(4,1)S(1)}, pred[4,12]{0,1:T(8,128)(4,1)S(1)},...) fusion(pred[]{:T(512)S(6)} %lt.129, ...), kind=kLoop, calls=%fused_computation.122 | loop fusion | flops 3503 | bytes 1377 | tf_op jit(solution)/shard_map/reduce_or | solution.py:23
  9.6 2.5 %select_reduce_fusion.9 = (s32[]{:T(128)}, s32[]{:T(128)}, s32[]{:T(128)}, s32[]{:T(128)}, s32[]{:T(128)}, /*index=5*/s32[]{:T(128)}, s32[]{:T(128)}, s32[]{:T(128)}, s32[4,12]{0,1:T(8,128)}, s32[4,12]{0,1:T(8,128)S(1)}) fusion(pred[4,12]{0,1:T(8,128)(4,1)S(1)} %get-tuple-element.63, pred[4,12]{0,1:T(8,128)(4,1)S(1)} %get-tuple-element.64, ...), kind=kLoop, calls=%fused_computation.88 | loop fusion | flops 3160 | bytes 2024 | tf_op jit(solution)/shard_map/reduce_min | solution.py:21
  16.0 1.4 %copy.17 = bf16[512,768]{0,1:T(8,128)(2,1)S(1)} copy(bf16[512,768]{1,0:T(8,128)(2,1)} %param.6) | data formatting | bytes 1572864 | tf_op args[1]
  17.4 0.0 copy-done
  17.4 0.3 copy.18
  17.7 0.4 fusion.19
  18.1 0.1 pad_maximum_fusion.2
  18.2 5.8 %collective-permute-start.1 = (bf16[2,256,768]{1,2,0:T(8,128)(2,1)S(1)}, bf16[2,256,768]{1,2,0:T(8,128)(2,1)}, u32[]{:S(2)}, u32[]{:S(2)}) collective-permute-start(bf16[2,256,768]{1,2,0:T(8,128)(2,1)S(1)} %pad_maximum_fusion.2), channel_id=1, source_target_pairs={{0,4},{4,8},{8,12},{12,16},{16,20},{20,24},{24,28},{1,5},{5,9},{9,... | collective-permute-start | bytes 2359304 | tf_op jit(solution)/shard_map/ppermute | solution.py:15
  24.0 1.0 pad_maximum_fusion.1
  24.9 3.5 %collective-permute-start = (bf16[2,256,768]{1,2,0:T(8,128)(2,1)}, bf16[2,256,768]{1,2,0:T(8,128)(2,1)}, u32[]{:S(2)}, u32[]{:S(2)}) collective-permute-start(bf16[2,256,768]{1,2,0:T(8,128)(2,1)} %pad_maximum_fusion.1), channel_id=1, source_target_pairs={{0,8},{4,12},{8,16},{12,20},{16,24},{20,28},{1,9},{5,13},{9,17},{1... | collective-permute-start | bytes 2359304 | tf_op jit(solution)/shard_map/ppermute | solution.py:15
  29.7 0.0 copy-start.3
  29.7 0.0 copy-start.4
  29.7 0.1 fusion.20
  29.9 1.0 pad_maximum_fusion.3
  30.9 0.0 copy-start.1
  30.9 1.4 %collective-permute-start.2 = (bf16[2,256,768]{1,2,0:T(8,128)(2,1)}, bf16[2,256,768]{1,2,0:T(8,128)(2,1)}, u32[]{:S(2)}, u32[]{:S(2)}) collective-permute-start(bf16[2,256,768]{1,2,0:T(8,128)(2,1)} %pad_maximum_fusion.3), channel_id=1, source_target_pairs={{4,0},{8,4},{12,8},{16,12},{20,16},{24,20},{28,24},{5,1},{9,5},{13... | collective-permute-start | bytes 2359304 | tf_op jit(solution)/shard_map/ppermute | solution.py:15
  32.3 1.0 pad_maximum_fusion.4
  33.3 1.5 %collective-permute-start.3 = (bf16[2,256,768]{1,2,0:T(8,128)(2,1)}, bf16[2,256,768]{1,2,0:T(8,128)(2,1)}, u32[]{:S(2)}, u32[]{:S(2)}) collective-permute-start(bf16[2,256,768]{1,2,0:T(8,128)(2,1)} %pad_maximum_fusion.4), channel_id=1, source_target_pairs={{8,0},{12,4},{16,8},{20,12},{24,16},{28,20},{9,1},{13,5},{17,9},{2... | collective-permute-start | bytes 2359304 | tf_op jit(solution)/shard_map/ppermute | solution.py:15
  34.7 0.7 fusion.34
  35.4 0.0 copy-done.3
  35.4 0.0 copy-done.4
  35.4 0.8 select_reduce_fusion
  49.9 0.7 reduce_or.45
  51.9 0.1 copy.19
  52.0 0.1 concatenate.23
  52.1 0.4 compare_reduce_fusion
  52.4 0.5 broadcast_in_dim.47
  52.9 1.3 copy.29
  54.2 0.0 copy-done.1
  54.2 1.2 copy.20
  55.4 0.1 fusion.9
  55.5 0.0 collective-permute-done
  55.5 1.2 constant_dynamic-update-slice_fusion.3
  56.7 0.0 collective-permute-done.1
  56.7 1.2 constant_dynamic-update-slice_fusion.2
  57.9 0.0 collective-permute-done.2
  57.9 1.2 constant_dynamic-update-slice_fusion.1
  59.1 10.7 %collective-permute-done.3 = bf16[2,256,768]{1,2,0:T(8,128)(2,1)} collective-permute-done((bf16[2,256,768]{1,2,0:T(8,128)(2,1)}, bf16[2,256,768]{1,2,0:T(8,128)(2,1)}, u32[]{:S(2)}, u32[]{:S(2)}) %collective-permute-start.3) | collective-permute-done | bytes 786464 | tf_op jit(solution)/shard_map/ppermute | solution.py:15
  69.8 1.2 constant_dynamic-update-slice_fusion
  71.0 0.0 copy-start.2
  71.0 1.7 %fusion.35 = (bf16[1,1536,768]{1,2,0:T(8,128)(2,1)}, bf16[1,1536,768]{1,2,0:T(8,128)(2,1)S(1)}) fusion(bf16[2,1536,768]{1,2,0:T(8,128)(2,1)S(1)} %constant_dynamic-update-slice_fusion), kind=kLoop, calls=%fused_computation.125 | loop fusion | bytes 9437184 | tf_op jit(solution)/shard_map/slice | solution.py:58
  72.7 0.0 copy-done.2
  72.7 12.9 %fusion.36 = (f32[6,512]{1,0:T(8,128)S(1)}, bf16[6,512,1536]{1,2,0:T(8,128)(2,1)}) fusion(pred[512,1536]{0,1:T(8,128)(4,1)S(1)} %bitcast.54, bf16[1536,6,128]{0,2,1:T(8,128)(2,1)} %bitcast.53, bf16[512,6,128]{0,2,1:T(8,128)(2,1)} %bitcast.55), kind=kOutput, calls=%fused_computation.126 | convolution fusion | flops 1236272640 | bytes 13381632 | tf_op jit(solution)/shard_map/sub | solution.py:65
  85.6 5.1 %fusion.10 = bf16[512,6,128]{0,2,1:T(8,128)(2,1)S(1)} fusion(bf16[1536,6,128]{0,2,1:T(8,128)(2,1)S(1)} %bitcast.52, bf16[6,512,1536]{1,2,0:T(8,128)(2,1)} %get-tuple-element.71, f32[512,6]{0,1:T(8,128)S(1)} %bitcast.57), kind=kOutput, calls=%fused_computation.31 | convolution fusion | flops 1208745984 | bytes 12595200 | tf_op jit(solution)/shard_map/hqk,khd->qhd/dot_general | solution.py:68
  90.7 6.4 %convolution_convert_fusion = bf16[512,3072]{1,0:T(8,128)(2,1)} fusion(bf16[512,768]{0,1:T(8,128)(2,1)S(1)} %bitcast.56, bf16[768,3072]{1,0:T(8,128)(2,1)} %param.9), kind=kOutput, calls=%fused_computation.9 | convolution fusion | flops 2417491968 | bytes 8650752 | tf_op jit(solution)/shard_map/dot_general | solution.py:75
  97.1 0.0 reduce-scatter.2.cloned.1.call-update
  97.1 35.5 %reduce-scatter.2.cloned.1.call-done = bf16[128,3072]{1,0:T(8,128)(2,1)} async-done(((bf16[512,3072]{1,0:T(8,128)(2,1)}), bf16[128,3072]{1,0:T(8,128)(2,1)}) %reduce-scatter.2.cloned.1.call-update) | async-done | bytes 786448 | tf_op jit(solution)/shard_map/reduce_scatter | solution.py:74
  (1 shorter events, 0.0 us)
Async XLA Ops:
  6.5 10.8 %copy-start = (bf16[512,768]{1,0:T(8,128)(2,1)S(1)}, bf16[512,768]{1,0:T(8,128)(2,1)}, u32[]{:S(2)}) copy-start(bf16[512,768]{1,0:T(8,128)(2,1)} %param.7) | copy-start | bytes 2359300
  6.5 126.0 %reduce-scatter.2.cloned.1.call-start = ((), (), s32[]{:S(2)}) async-start(), calls=%async_computation.1 | async-start | bytes 3932160 | tf_op jit(solution)/shard_map/reduce_scatter | solution.py:74
  18.2 38.5 %collective-permute-start.1 = (bf16[2,256,768]{1,2,0:T(8,128)(2,1)S(1)}, bf16[2,256,768]{1,2,0:T(8,128)(2,1)}, u32[]{:S(2)}, u32[]{:S(2)}) collective-permute-start(bf16[2,256,768]{1,2,0:T(8,128)(2,1)S(1)} %pad_maximum_fusion.2), channel_id=1, source_target_pairs={{0,4},{4,8},{8,12},{12,16},{16,20},{20,24},{24,28},{1,5},{5,9},{9,... | collective-permute-start | bytes 2359304 | tf_op jit(solution)/shard_map/ppermute | solution.py:15
  24.9 30.5 %collective-permute-start = (bf16[2,256,768]{1,2,0:T(8,128)(2,1)}, bf16[2,256,768]{1,2,0:T(8,128)(2,1)}, u32[]{:S(2)}, u32[]{:S(2)}) collective-permute-start(bf16[2,256,768]{1,2,0:T(8,128)(2,1)} %pad_maximum_fusion.1), channel_id=1, source_target_pairs={{0,8},{4,12},{8,16},{12,20},{16,24},{20,28},{1,9},{5,13},{9,17},{1... | collective-permute-start | bytes 2359304 | tf_op jit(solution)/shard_map/ppermute | solution.py:15
  29.7 5.7 %copy-start.3 = (s32[4,12]{0,1:T(8,128)S(1)}, s32[4,12]{0,1:T(8,128)}, u32[]{:S(2)}) copy-start(s32[4,12]{0,1:T(8,128)} %get-tuple-element.62) | copy-start | bytes 580
  29.7 5.7 %copy-start.4 = (pred[4,12]{0,1:T(8,128)(4,1)S(1)}, pred[4,12]{0,1:T(8,128)(4,1)}, u32[]{:S(2)}) copy-start(pred[4,12]{0,1:T(8,128)(4,1)} %get-tuple-element.34) | copy-start | bytes 148
  30.9 23.3 %copy-start.1 = (bf16[512,768]{1,0:T(8,128)(2,1)S(1)}, bf16[512,768]{1,0:T(8,128)(2,1)}, u32[]{:S(2)}) copy-start(bf16[512,768]{1,0:T(8,128)(2,1)} %param.5) | copy-start | bytes 2359300
  30.9 27.1 %collective-permute-start.2 = (bf16[2,256,768]{1,2,0:T(8,128)(2,1)}, bf16[2,256,768]{1,2,0:T(8,128)(2,1)}, u32[]{:S(2)}, u32[]{:S(2)}) collective-permute-start(bf16[2,256,768]{1,2,0:T(8,128)(2,1)} %pad_maximum_fusion.3), channel_id=1, source_target_pairs={{4,0},{8,4},{12,8},{16,12},{20,16},{24,20},{28,24},{5,1},{9,5},{13... | collective-permute-start | bytes 2359304 | tf_op jit(solution)/shard_map/ppermute | solution.py:15
  33.3 36.5 %collective-permute-start.3 = (bf16[2,256,768]{1,2,0:T(8,128)(2,1)}, bf16[2,256,768]{1,2,0:T(8,128)(2,1)}, u32[]{:S(2)}, u32[]{:S(2)}) collective-permute-start(bf16[2,256,768]{1,2,0:T(8,128)(2,1)} %pad_maximum_fusion.4), channel_id=1, source_target_pairs={{8,0},{12,4},{16,8},{20,12},{24,16},{28,20},{9,1},{13,5},{17,9},{2... | collective-permute-start | bytes 2359304 | tf_op jit(solution)/shard_map/ppermute | solution.py:15
  71.0 1.7 %copy-start.2 = (pred[192,8,4,128]{3,1,2,0:T(8,128)(4,1)S(1)}, pred[192,8,4,128]{3,1,2,0:T(8,128)(4,1)}, u32[]{:S(2)}) copy-start(pred[192,8,4,128]{3,1,2,0:T(8,128)(4,1)} %copy.29) | copy-start | bytes 2359300
Sparse Core Ops, SparseCore 0:
  97.2 35.2 reduce-scatter.1

commit v2 on v0

v2 whole, which is shorter than its diff:
```python
import functools
import math

import jax
import jax.numpy as jnp
from jax import lax
from jax.experimental import pallas as pl
from jax.experimental.pallas import tpu as pltpu
from jax.sharding import PartitionSpec as P

HD = 128
TILE = 128
REACH = 2
PAIR = 2
OFFSETS = tuple(o for o in range(-REACH, REACH + 1) if o)
MASKED = -1e30
MESH = pl.DeviceIdType.MESH


def dot(a, b, contract):
    return lax.dot_general(a, b, (((1,), (contract,)), ((), ())), preferred_element_type=jnp.float32)


def kernel(devices, groups, chunk, ids, bias, q, k, v, w, out,
           packed, halo, ctx, ctx_mate, w_own, w_mate, part_out, part_in, own,
           halo_send, halo_recv, ctx_send, ctx_recv, part_send, part_recv, w_sems):
    device, group = lax.axis_index("ctx"), lax.axis_index("head")
    parity, place = group % 2, group // 2
    mate = group + 1 - 2 * parity
    tokens, columns = q.shape
    heads, tiles = columns // HD, tokens // TILE
    width = out.shape[1]
    rows = tokens // groups
    pairs = groups // 2
    chunks = width // chunk

    def reader(slot):
        return device - OFFSETS[slot]

    def source(slot):
        return device + OFFSETS[slot]

    def inside(index):
        return (index >= 0) & (index < devices)

    barrier = pltpu.get_barrier_semaphore()
    expected = jnp.int32(pairs)
    for slot in range(len(OFFSETS)):
        @pl.when(inside(reader(slot)))
        def _(slot=slot):
            pl.semaphore_signal(barrier, 1, device_id=(reader(slot), group), device_id_type=MESH)
        expected = expected + inside(source(slot)).astype(jnp.int32)
    pl.semaphore_signal(barrier, 1, device_id=(device, mate), device_id_type=MESH)
    for step in range(1, pairs):
        peer = 2 * ((place + step) % pairs) + parity
        pl.semaphore_signal(barrier, 1, device_id=(device, peer), device_id_type=MESH)

    load_w = pltpu.make_async_copy(w, w_own, w_sems.at[0])
    load_w.start()

    for slot in range(len(OFFSETS)):
        for which in range(PAIR):
            picked = ids[PAIR * slot + which]
            for side, ref in ((0, k), (1, v)):
                tile = ref[picked]
                for h in range(heads):
                    packed[h, slot, side, which * TILE:(which + 1) * TILE, :] = tile[:, h * HD:(h + 1) * HD]
    for slot in range(len(OFFSETS)):
        @pl.when(jnp.logical_not(inside(source(slot))))
        def _(slot=slot):
            halo[:, :, slot] = jnp.zeros((heads, 2, PAIR * TILE, HD), halo.dtype)

    pl.semaphore_wait(barrier, expected)

    def halo_copy(h, slot):
        return pltpu.make_async_remote_copy(
            src_ref=packed.at[h, slot], dst_ref=halo.at[h, :, slot],
            send_sem=halo_send.at[h, slot], recv_sem=halo_recv.at[h, slot],
            device_id=(reader(slot), group), device_id_type=MESH)

    def each_send(act):
        def one(h, carry):
            for slot in range(len(OFFSETS)):
                @pl.when(inside(reader(slot)))
                def _(slot=slot):
                    act(halo_copy(h, slot))
            return carry
        lax.fori_loop(0, heads, one, 0)

    each_send(lambda copy: copy.start())
    send_w = pltpu.make_async_remote_copy(
        src_ref=w, dst_ref=w_mate, send_sem=w_sems.at[1], recv_sem=w_sems.at[2],
        device_id=(device, mate), device_id_type=MESH)
    send_w.start()

    def ctx_copy(h, i):
        block = pl.multiple_of((2 * i + 1 - parity) * rows, rows)
        lanes = pl.ds(pl.multiple_of(h * HD, HD), HD)
        return pltpu.make_async_remote_copy(
            src_ref=ctx.at[pl.ds(block, rows), lanes],
            dst_ref=ctx_mate.at[pl.ds(i * rows, rows), lanes],
            send_sem=ctx_send.at[h, i], recv_sem=ctx_recv.at[h, i],
            device_id=(device, mate), device_id_type=MESH)

    scale = HD ** -0.5 * math.log2(math.e)
    near = tokens

    def one_head(h, carry):
        for slot in range(len(OFFSETS)):
            @pl.when(inside(source(slot)))
            def _(slot=slot):
                halo_copy(h, slot).wait_recv()
        lanes = pl.ds(pl.multiple_of(h * HD, HD), HD)
        k_own, v_own = k[:, :, lanes].reshape(tokens, HD), v[:, :, lanes].reshape(tokens, HD)
        k_far = halo[h, 0].reshape(len(OFFSETS) * PAIR * TILE, HD)
        v_far = halo[h, 1].reshape(len(OFFSETS) * PAIR * TILE, HD)
        for i in range(tiles):
            half = tiles // 2
            t = 2 * i + 1 - parity if i < half else 2 * (i - half) + parity
            span = pl.ds(pl.multiple_of(t * TILE, TILE), TILE)
            qt = q[span, lanes]
            shift = bias[pl.ds(t, 1), :]
            s_own = dot(qt, k_own, 1) * scale + shift[:, :near]
            s_far = dot(qt, k_far, 1) * scale + shift[:, near:]
            top = jnp.maximum(jnp.max(s_own, axis=1, keepdims=True), jnp.max(s_far, axis=1, keepdims=True))
            p_own, p_far = jnp.exp2(s_own - top), jnp.exp2(s_far - top)
            total = jnp.sum(p_own, axis=1, keepdims=True) + jnp.sum(p_far, axis=1, keepdims=True)
            summed = dot(p_own.astype(jnp.bfloat16), v_own, 0) + dot(p_far.astype(jnp.bfloat16), v_far, 0)
            ctx[span, lanes] = (summed * (1.0 / total)).astype(ctx.dtype)
            if i == (half if rows == TILE and half < tiles else tiles - 1):
                for j in range(pairs):
                    ctx_copy(h, j).start()
        return carry

    lax.fori_loop(0, heads, one_head, 0)

    load_w.wait()
    send_w.wait_recv()

    def wait_ctx(h, carry):
        for j in range(pairs):
            ctx_copy(h, j).wait_recv()
        return carry
    lax.fori_loop(0, heads, wait_ctx, 0)

    def project(i, c):
        mine = ctx[pl.ds(pl.multiple_of((2 * i + parity) * rows, rows), rows), :]
        other = ctx_mate[pl.ds(pl.multiple_of(i * rows, rows), rows), :]
        cols = pl.ds(c * chunk, chunk)
        return dot(mine, w_own[:, cols], 0) + dot(other, w_mate[:, cols], 0)

    def part_copy(step, c):
        peer = 2 * ((place + step) % pairs) + parity
        cols = pl.ds(c * chunk, chunk)
        return pltpu.make_async_remote_copy(
            src_ref=part_out.at[step - 1, c], dst_ref=part_in.at[step - 1, c],
            send_sem=part_send.at[step - 1, c], recv_sem=part_recv.at[step - 1, c],
            device_id=(device, peer), device_id_type=MESH)

    waiting = None
    for step in range(1, pairs):
        for c in range(chunks):
            part_out[step - 1, c] = project((place + step) % pairs, c).astype(part_out.dtype)
            if waiting is not None:
                part_copy(*waiting).start()
            waiting = (step, c)
    for c in range(chunks):
        own[c] = project(place, c)
        if waiting is not None:
            part_copy(*waiting).start()
            waiting = None
    for c in range(chunks):
        total = own[c]
        for step in range(1, pairs):
            part_copy(step, c).wait_recv()
            total = total + part_in[step - 1, c].astype(jnp.float32)
        out[:, c * chunk:(c + 1) * chunk] = total.astype(out.dtype)

    each_send(lambda copy: copy.wait_send())
    send_w.wait_send()

    def drain_ctx(h, carry):
        for j in range(pairs):
            ctx_copy(h, j).wait_send()
        return carry
    lax.fori_loop(0, heads, drain_ctx, 0)
    for step in range(1, pairs):
        for c in range(chunks):
            part_copy(step, c).wait_send()


def plan(kv_tiles, per):
    device = lax.axis_index("ctx")
    shifts = jnp.array(OFFSETS, jnp.int32)
    near = jnp.full_like(shifts, device)
    readers = jnp.concatenate([device - shifts, near])[:, None, None]
    owners = jnp.concatenate([near, device + shifts])[:, None, None]
    home = lax.broadcasted_iota(jnp.int32, kv_tiles.shape, 0) // per
    local = kv_tiles % per
    read = (home == readers) & (kv_tiles // per == owners)
    least = jnp.min(jnp.where(read, local, per), axis=(1, 2))
    most = jnp.max(jnp.where(read, local, -1), axis=(1, 2))
    count = len(OFFSETS)
    ids = jnp.stack([jnp.minimum(least[:count], per - 1), jnp.maximum(most[:count], 0)], axis=1)
    least, most, base = least[count:], most[count:], (device + shifts) * per
    far = jnp.stack(
        [jnp.where(least < per, base + least, -1), jnp.where(most > least, base + most, -1)], axis=1
    )
    listed = jnp.concatenate([device * per + jnp.arange(per, dtype=jnp.int32), far.reshape(-1)])
    mine = lax.dynamic_slice_in_dim(kv_tiles, device * per, per, 0)
    allowed = jnp.any(mine[:, None, :] == listed[None, :, None], axis=2)
    bias = jnp.where(allowed, 0.0, MASKED).astype(jnp.float32)
    bias = jnp.broadcast_to(bias[:, :, None], bias.shape + (TILE,)).reshape(per, -1)
    return ids.reshape(-1), bias


def body(queries, keys, values, kv_tiles, out_weight):
    tokens, columns = queries.shape
    width = out_weight.shape[1]
    devices, groups = lax.axis_size("ctx"), lax.axis_size("head")
    heads, rows, pairs, slots = columns // HD, tokens // groups, groups // 2, len(OFFSETS)
    chunk = min(width, 512)
    chunks = width // chunk
    ids, bias = plan(kv_tiles, tokens // TILE)
    vmem = pl.BlockSpec(memory_space=pltpu.VMEM)
    sems = pltpu.SemaphoreType.DMA
    bf16 = jnp.bfloat16
    return pl.pallas_call(
        functools.partial(kernel, devices, groups, chunk),
        out_shape=jax.ShapeDtypeStruct((rows, width), bf16),
        in_specs=[pl.BlockSpec(memory_space=pltpu.SMEM), vmem, vmem, vmem, vmem,
                  pl.BlockSpec(memory_space=pl.ANY)],
        out_specs=vmem,
        scratch_shapes=[
            pltpu.VMEM((heads, slots, 2, PAIR * TILE, HD), bf16),
            pltpu.VMEM((heads, 2, slots, PAIR * TILE, HD), bf16),
            pltpu.VMEM((tokens, columns), bf16),
            pltpu.VMEM((pairs * rows, columns), bf16),
            pltpu.VMEM((columns, width), bf16),
            pltpu.VMEM((columns, width), bf16),
            pltpu.VMEM((pairs - 1, chunks, rows, chunk), bf16),
            pltpu.VMEM((pairs - 1, chunks, rows, chunk), bf16),
            pltpu.VMEM((chunks, rows, chunk), jnp.float32),
            sems((heads, slots)), sems((heads, slots)),
            sems((heads, pairs)), sems((heads, pairs)),
            sems((pairs - 1, chunks)), sems((pairs - 1, chunks)),
            sems((3,)),
        ],
        compiler_params=pltpu.CompilerParams(
            collective_id=0, has_side_effects=True, vmem_limit_bytes=56 * 2 ** 20),
    )(ids, bias, queries, keys.reshape(-1, TILE, columns), values.reshape(-1, TILE, columns), out_weight)


def solution(mesh):
    return jax.shard_map(
        body,
        mesh=mesh,
        in_specs=(P("ctx", "head"), P("ctx", "head"), P("ctx", "head"), P(), P("head", None)),
        out_specs=P(("ctx", "head"), None),
        check_vma=False,
    )
```

time: 181 us -> 72.6 us (0.40)
  waiting for transfers between devices: 93.8 us -> 0 us
  Pallas kernels: 0 us -> 64.7 us
  matrix products: 36.2 us -> 0 us
  local copies, waits for them, and re-layouts: 21.8 us -> 4.74 us
  between operations: 13.5 us -> 0.03 us
  starting transfers between devices: 13.2 us -> 0 us
    pallas_call x0 -> x1, Pallas kernels: none -> 64.7 us  [body(): pl.pallas_call(functools.partial(kernel, devices, groups, chunk), out_sha...]
    ppermute x4 -> x0, waiting for transfers between devices: 55.7 us -> none  [shifted(): return lax.ppermute(value, axis, pairs)]
    reduce_scatter x1 -> x0, waiting for transfers between devices: 38.1 us -> none  [body(): lax.psum_scatter(jnp.dot(context, out_weight, preferred_element_type=jnp....]
    sub x1 -> x0, matrix products: 20.9 us -> none  [body(): weights = jnp.where(allowed_keys[None], jnp.exp(masked - row_max), 0.0)]
    dot_general x2 -> x0, matrix products: 15.2 us -> none  [the longest x1 8.86 us: body(): jnp.einsum('hqk,khd->qhd', rounded, value_heads, preferred_element_type=j...]
    ppermute x4 -> x0, starting transfers between devices: 13.2 us -> none  [shifted(): return lax.ppermute(value, axis, pairs)]
    unnamed x13 -> x3, local copies, waits for them, and re-layouts: 13.7 us -> 2.76 us
    slice x1 -> x0, local copies, waits for them, and re-layouts: 5.78 us -> none  [body(): key_heads = buffer[0].reshape(key_tiles * TILE, heads_here, HD)]
  transfers between devices with their start and end apart: 5 -> 0, of which waited for: 3 -> 0; matrix products, arithmetic and copies ran while one was open for 7% -> 0% of each run, Pallas kernels for 0% -> 0%
where the time goes in v2:
time: 72.6 us; the launch traced here: 72.3 us
  Pallas kernels  64.7 us (89%)
  local copies, waits for them, and re-layouts  4.74 us (7%)
  other arithmetic  2.84 us (4%)
    pallas_call x1, Pallas kernels, body(): pl.pallas_call(functools.partial(kernel, devices, groups, chunk), out_sha...  64.7 us
    unnamed x3, local copies, waits for them, and re-layouts  2.76 us

profile of v2, /device:TPU:0, one launch (start us, length us, event | category | flops | bytes accessed | tf_op | source)
XLA Modules:
  0.0 72.3 jit_solution(9935539613532995657)
XLA Ops:
  0.0 0.7 broadcast_add_fusion
  0.7 0.1 concatenate.10
  0.8 0.8 %constant_dynamic-slice_fusion = s32[4,12]{0,1:T(8,128)S(1)} fusion(s32[32,12]{0,1:T(8,128)} %param.9, s32[]{:T(128)S(6)} %select_n.49), kind=kLoop, calls=%fused_computation.33 | loop fusion | bytes 388 | tf_op jit(solution)/shard_map/dynamic_slice | solution.py:210
  1.6 0.1 copy.18
  1.7 0.7 add_select_fusion.1
  2.4 0.2 select_reduce_fusion.1
  2.6 0.7 %fusion.2 = (s32[4,1]{0,1:T(1,128)S(1)}, s32[4,1]{0,1:T(1,128)S(1)}, s32[4,1]{0,1:T(1,128)S(1)}, s32[4,1]{0,1:T(1,128)S(1)}) fusion(s32[8]{0:T(128)S(1)} %get-tuple-element.5, s32[4]{0:T(128)} %constant.64.clone, s32[]{:T(128)S(6)} %axis_index.15, s32[8]{0:T(128)S(1)} %get-tuple-element.6), kind=kLoop, calls=%fused_computation.24 | loop fusion | flops 40 | bytes 148 | tf_op jit(solution)/shard_map/stack | solution.py:206
  3.3 0.1 copy.19
  3.4 0.1 reshape.56
  3.5 0.1 pad_add_fusion.2
  3.6 0.4 compare_reduce_fusion
  4.0 0.1 copy.17
  4.1 0.7 reshape.55.ids
  4.7 0.1 copy.20
  4.8 0.1 broadcast_bitcast_fusion
  4.9 0.6 copy.23
  5.5 64.7 %shard_map.64 = bf16[128,3072]{1,0:T(8,128)(2,1)} custom-call(s32[8]{0:T(128)} %reshape.55.ids, f32[4,1536]{1,0:T(4,128)} %bitcast.17, bf16[512,768]{1,0:T(8,128)(2,1)} %q.1, bf16[4,128,768]{2,1,0:T(8,128)(2,1)} %bitcast.15, bf16[4,128,768]{2,1,0:T(8,128)(2,1)} %bitcast.16, bf16[768,3072]{1,0:T(8,128)(2,1)} %w.1), custom_call_target="tpu_custom_call" | custom-call | tf_op jit(solution)/shard_map/pallas_call | solution.py:228
  70.3 2.1 %copy.25 = bf16[128,3072]{1,0:T(8,128)(2,1)} copy(bf16[128,3072]{1,0:T(8,128)(2,1)} %shard_map.64) | data formatting | bytes 1572864
  (8 shorter events, 0.0 us)

commit v3 on v2

--- a/solution.py
+++ b/solution.py
@@ -21,8 +21,8 @@
     return lax.dot_general(a, b, (((1,), (contract,)), ((), ())), preferred_element_type=jnp.float32)
 
 
-def kernel(devices, groups, chunk, ids, bias, q, k, v, w, out,
-           packed, halo, ctx, ctx_mate, w_own, w_mate, part_out, part_in, own,
+def kernel(devices, groups, chunk, lists, q, k, v, w, out,
+           bias, packed, halo, ctx, ctx_mate, w_own, w_mate, part_out, part_in, own,
            halo_send, halo_recv, ctx_send, ctx_recv, part_send, part_recv, w_sems):
     device, group = lax.axis_index("ctx"), lax.axis_index("head")
     parity, place = group % 2, group // 2
@@ -58,6 +58,21 @@
     load_w = pltpu.make_async_copy(w, w_own, w_sems.at[0])
     load_w.start()
 
+    entries = lists.shape[0]
+
+    def sent(r, found):
+        found = list(found)
+        for slot in range(len(OFFSETS)):
+            row = (reader(slot) + devices) % devices * tiles + r
+            for e in range(entries):
+                x = lists[e, row] - device * tiles
+                least, most = found[2 * slot], found[2 * slot + 1]
+                found[2 * slot] = jnp.minimum(least, jnp.where(x < 0, tiles - 1, x))
+                found[2 * slot + 1] = jnp.maximum(most, jnp.where(x >= tiles, 0, x))
+        return tuple(found)
+
+    ids = lax.fori_loop(0, tiles, sent, (jnp.int32(tiles - 1), jnp.int32(0)) * len(OFFSETS))
+
     for slot in range(len(OFFSETS)):
         for which in range(PAIR):
             picked = ids[PAIR * slot + which]
@@ -92,6 +107,35 @@
         src_ref=w, dst_ref=w_mate, send_sem=w_sems.at[1], recv_sem=w_sems.at[2],
         device_id=(device, mate), device_id_type=MESH)
     send_w.start()
+
+    def received(r, found):
+        found = list(found)
+        for e in range(entries):
+            tile = lists[e, device * tiles + r]
+            for slot in range(len(OFFSETS)):
+                x = tile - source(slot) * tiles
+                least, most = found[2 * slot], found[2 * slot + 1]
+                found[2 * slot] = jnp.minimum(least, jnp.where(x < 0, tiles, x))
+                found[2 * slot + 1] = jnp.maximum(most, jnp.where(x >= tiles, -1, x))
+        return tuple(found)
+
+    found = lax.fori_loop(0, tiles, received, (jnp.int32(tiles), jnp.int32(-1)) * len(OFFSETS))
+    listed = [device * tiles + j for j in range(tiles)]
+    for slot in range(len(OFFSETS)):
+        least, most = found[2 * slot], found[2 * slot + 1]
+        listed.append(jnp.where(least < tiles, source(slot) * tiles + least, -1))
+        listed.append(jnp.where(most > least, source(slot) * tiles + most, -1))
+
+    def mask(t, carry):
+        added = [jnp.float32(MASKED)] * len(listed)
+        for e in range(entries):
+            tile = lists[e, device * tiles + t]
+            added = [jnp.where(tile == other, 0.0, value) for other, value in zip(listed, added)]
+        for j, value in enumerate(added):
+            bias[t, :, j * TILE:(j + 1) * TILE] = jnp.full((1, TILE), value, jnp.float32)
+        return carry
+
+    lax.fori_loop(0, tiles, mask, 0)
 
     def ctx_copy(h, i):
         block = pl.multiple_of((2 * i + 1 - parity) * rows, rows)
@@ -119,7 +163,7 @@
             t = 2 * i + 1 - parity if i < half else 2 * (i - half) + parity
             span = pl.ds(pl.multiple_of(t * TILE, TILE), TILE)
             qt = q[span, lanes]
-            shift = bias[pl.ds(t, 1), :]
+            shift = bias[t]
             s_own = dot(qt, k_own, 1) * scale + shift[:, :near]
             s_far = dot(qt, k_far, 1) * scale + shift[:, near:]
             top = jnp.maximum(jnp.max(s_own, axis=1, keepdims=True), jnp.max(s_far, axis=1, keepdims=True))
@@ -189,31 +233,6 @@
             part_copy(step, c).wait_send()
 
 
-def plan(kv_tiles, per):
-    device = lax.axis_index("ctx")
-    shifts = jnp.array(OFFSETS, jnp.int32)
-    near = jnp.full_like(shifts, device)
-    readers = jnp.concatenate([device - shifts, near])[:, None, None]
-    owners = jnp.concatenate([near, device + shifts])[:, None, None]
-    home = lax.broadcasted_iota(jnp.int32, kv_tiles.shape, 0) // per
-    local = kv_tiles % per
-    read = (home == readers) & (kv_tiles // per == owners)
-    least = jnp.min(jnp.where(read, local, per), axis=(1, 2))
-    most = jnp.max(jnp.where(read, local, -1), axis=(1, 2))
-    count = len(OFFSETS)
-    ids = jnp.stack([jnp.minimum(least[:count], per - 1), jnp.maximum(most[:count], 0)], axis=1)
-    least, most, base = least[count:], most[count:], (device + shifts) * per
-    far = jnp.stack(
-        [jnp.where(least < per, base + least, -1), jnp.where(most > least, base + most, -1)], axis=1
-    )
-    listed = jnp.concatenate([device * per + jnp.arange(per, dtype=jnp.int32), far.reshape(-1)])
-    mine = lax.dynamic_slice_in_dim(kv_tiles, device * per, per, 0)
-    allowed = jnp.any(mine[:, None, :] == listed[None, :, None], axis=2)
-    bias = jnp.where(allowed, 0.0, MASKED).astype(jnp.float32)
-    bias = jnp.broadcast_to(bias[:, :, None], bias.shape + (TILE,)).reshape(per, -1)
-    return ids.reshape(-1), bias
-
-
 def body(queries, keys, values, kv_tiles, out_weight):
     tokens, columns = queries.shape
     width = out_weight.shape[1]
@@ -221,17 +240,17 @@
     heads, rows, pairs, slots = columns // HD, tokens // groups, groups // 2, len(OFFSETS)
     chunk = min(width, 512)
     chunks = width // chunk
-    ids, bias = plan(kv_tiles, tokens // TILE)
     vmem = pl.BlockSpec(memory_space=pltpu.VMEM)
     sems = pltpu.SemaphoreType.DMA
     bf16 = jnp.bfloat16
     return pl.pallas_call(
         functools.partial(kernel, devices, groups, chunk),
         out_shape=jax.ShapeDtypeStruct((rows, width), bf16),
-        in_specs=[pl.BlockSpec(memory_space=pltpu.SMEM), vmem, vmem, vmem, vmem,
+        in_specs=[pl.BlockSpec(memory_space=pltpu.SMEM), vmem, vmem, vmem,
                   pl.BlockSpec(memory_space=pl.ANY)],
         out_specs=vmem,
         scratch_shapes=[
+            pltpu.VMEM((tokens // TILE, 1, tokens + slots * PAIR * TILE), jnp.float32),
             pltpu.VMEM((heads, slots, 2, PAIR * TILE, HD), bf16),
             pltpu.VMEM((heads, 2, slots, PAIR * TILE, HD), bf16),
             pltpu.VMEM((tokens, columns), bf16),
@@ -248,7 +267,7 @@
         ],
         compiler_params=pltpu.CompilerParams(
             collective_id=0, has_side_effects=True, vmem_limit_bytes=56 * 2 ** 20),
-    )(ids, bias, queries, keys.reshape(-1, TILE, columns), values.reshape(-1, TILE, columns), out_weight)
+    )(kv_tiles.T, queries, keys.reshape(-1, TILE, columns), values.reshape(-1, TILE, columns), out_weight)
 
 
 def solution(mesh):

time: 72.6 us -> 67 us (0.923)
  other arithmetic: 2.84 us -> 0 us
  local copies, waits for them, and re-layouts: 4.74 us -> 2.06 us
    dynamic_slice x2 -> x0, local copies, waits for them, and re-layouts: 0.87 us -> none  [plan(): mine = lax.dynamic_slice_in_dim(kv_tiles, device * per, per, 0)]
    another operation x3 -> x0, other arithmetic: 0.75 us -> none  [the longest x2 0.74 us: plan(): jnp.stack([jnp.where(least < per, base + least, -1), jnp.where(most > lea...]
    reshape x2 -> x0, local copies, waits for them, and re-layouts: 0.75 us -> none  [the longest x1 0.66 us: plan(): return (ids.reshape(-1), bias)]
    unnamed x3 -> x1, local copies, waits for them, and re-layouts: 2.76 us -> 2.06 us
where the time goes in v3:
time: 67 us; the launch traced here: 66.8 us
  Pallas kernels  64.8 us (97%)
  local copies, waits for them, and re-layouts  2.06 us (3%)
    pallas_call x1, Pallas kernels, body(): pl.pallas_call(functools.partial(kernel, devices, groups, chunk), out_sha...  64.8 us
    unnamed x1, local copies, waits for them, and re-layouts  2.06 us

profile of v3, /device:TPU:0, one launch (start us, length us, event | category | flops | bytes accessed | tf_op | source)
XLA Modules:
  0.0 66.8 jit_solution(14269802867171075669)
XLA Ops:
  0.0 64.8 %shard_map.55 = bf16[128,3072]{1,0:T(8,128)(2,1)} custom-call(s32[12,32]{1,0:T(8,128)} %bitcast.5, bf16[512,768]{1,0:T(8,128)(2,1)} %q.1, bf16[4,128,768]{2,1,0:T(8,128)(2,1)} %bitcast.3, bf16[4,128,768]{2,1,0:T(8,128)(2,1)} %bitcast.4, bf16[768,3072]{1,0:T(8,128)(2,1)} %w.1), custom_call_target="tpu_custom_call" | custom-call | tf_op jit(solution)/shard_map/pallas_call | solution.py:246
  64.8 2.1 %copy.7 = bf16[128,3072]{1,0:T(8,128)(2,1)} copy(bf16[128,3072]{1,0:T(8,128)(2,1)} %shard_map.55) | data formatting | bytes 1572864

commit v4 on v3

--- a/solution.py
+++ b/solution.py
@@ -73,13 +73,14 @@
 
     ids = lax.fori_loop(0, tiles, sent, (jnp.int32(tiles - 1), jnp.int32(0)) * len(OFFSETS))
 
-    for slot in range(len(OFFSETS)):
-        for which in range(PAIR):
-            picked = ids[PAIR * slot + which]
-            for side, ref in ((0, k), (1, v)):
-                tile = ref[picked]
-                for h in range(heads):
+    def pack(h):
+        for slot in range(len(OFFSETS)):
+            for which in range(PAIR):
+                for side, ref in ((0, k), (1, v)):
+                    tile = ref[ids[PAIR * slot + which]]
                     packed[h, slot, side, which * TILE:(which + 1) * TILE, :] = tile[:, h * HD:(h + 1) * HD]
+
+    pack(0)
     for slot in range(len(OFFSETS)):
         @pl.when(jnp.logical_not(inside(source(slot))))
         def _(slot=slot):
@@ -93,16 +94,16 @@
             send_sem=halo_send.at[h, slot], recv_sem=halo_recv.at[h, slot],
             device_id=(reader(slot), group), device_id_type=MESH)
 
-    def each_send(act):
-        def one(h, carry):
-            for slot in range(len(OFFSETS)):
-                @pl.when(inside(reader(slot)))
-                def _(slot=slot):
-                    act(halo_copy(h, slot))
-            return carry
-        lax.fori_loop(0, heads, one, 0)
-
-    each_send(lambda copy: copy.start())
+    def send(h, act):
+        for slot in range(len(OFFSETS)):
+            @pl.when(inside(reader(slot)))
+            def _(slot=slot):
+                act(halo_copy(h, slot))
+
+    for h in range(heads):
+        if h + 1 < heads:
+            pack(h + 1)
+        send(h, lambda copy: copy.start())
     send_w = pltpu.make_async_remote_copy(
         src_ref=w, dst_ref=w_mate, send_sem=w_sems.at[1], recv_sem=w_sems.at[2],
         device_id=(device, mate), device_id_type=MESH)
@@ -220,7 +221,10 @@
             total = total + part_in[step - 1, c].astype(jnp.float32)
         out[:, c * chunk:(c + 1) * chunk] = total.astype(out.dtype)
 
-    each_send(lambda copy: copy.wait_send())
+    def drain_halo(h, carry):
+        send(h, lambda copy: copy.wait_send())
+        return carry
+    lax.fori_loop(0, heads, drain_halo, 0)
     send_w.wait_send()
 
     def drain_ctx(h, carry):
@@ -238,7 +242,7 @@
     width = out_weight.shape[1]
     devices, groups = lax.axis_size("ctx"), lax.axis_size("head")
     heads, rows, pairs, slots = columns // HD, tokens // groups, groups // 2, len(OFFSETS)
-    chunk = min(width, 512)
+    chunk = min(width, 256)
     chunks = width // chunk
     vmem = pl.BlockSpec(memory_space=pltpu.VMEM)
     sems = pltpu.SemaphoreType.DMA

time: 67 us -> 67 us (level)
  no operation moved by 1% of the time
where the time goes in v4:
time: 67 us; the launch traced here: 66.9 us
  Pallas kernels  64.8 us (97%)
  local copies, waits for them, and re-layouts  2.06 us (3%)
    pallas_call x1, Pallas kernels, body(): pl.pallas_call(functools.partial(kernel, devices, groups, chunk), out_sha...  64.8 us
    unnamed x1, local copies, waits for them, and re-layouts  2.06 us

profile of v4, /device:TPU:0, one launch (start us, length us, event | category | flops | bytes accessed | tf_op | source)
XLA Modules:
  0.0 66.9 jit_solution(2103950180655057689)
XLA Ops:
  0.0 64.8 %shard_map.55 = bf16[128,3072]{1,0:T(8,128)(2,1)} custom-call(s32[12,32]{1,0:T(8,128)} %bitcast.5, bf16[512,768]{1,0:T(8,128)(2,1)} %q.1, bf16[4,128,768]{2,1,0:T(8,128)(2,1)} %bitcast.3, bf16[4,128,768]{2,1,0:T(8,128)(2,1)} %bitcast.4, bf16[768,3072]{1,0:T(8,128)(2,1)} %w.1), custom_call_target="tpu_custom_call" | custom-call | tf_op jit(solution)/shard_map/pallas_call | solution.py:250
  64.8 2.1 %copy.7 = bf16[128,3072]{1,0:T(8,128)(2,1)} copy(bf16[128,3072]{1,0:T(8,128)(2,1)} %shard_map.55) | data formatting | bytes 1572864
